TPU v7x, 32 devices: a whole 2x2x4 slice. The times are simulated.
32 devices in a mesh: grp: 2 (over x), freq: 16 (over z, y, core).
Axes of the slice: x: 2, y: 2, z: 4, core: 2. Of those that a mesh axis runs over, the one named last changes fastest.
Arguments:
- start_field: bfloat16 [512, 384, 512], P(('grp', 'freq')), parts along dimension 0, may hold values from -2.390625 to 2.390625
- recorded: bfloat16 [32, 384, 4, 128], P(('grp', 'freq')), parts along dimension 0, may hold values from -6 to 6
- multiples: bfloat16 [32, 4, 3, 64, 128], P(('grp', 'freq')), parts along dimension 0, may hold values from -0.3125 to 0.3125
- block_index: int32 [4, 3], replicated, may hold values from 0 to 3, all different within a row
- radius: int32 [512, 384], P(('grp', 'freq')), parts along dimension 0, may hold values from 0 to 4
Outputs:
- field: float32 [512, 384, 512], P(('grp', 'freq')), parts along dimension 0
- residual: float32 [32, 384, 4, 128], P(('grp', 'freq')), parts along dimension 0
There are 2 independent parts, one for each index of `grp`. A program takes and returns all parts, laid end to end along the dimension named above; an argument that names none is the same for every part. Nothing has to cross between parts.
Inputs may be any that keep to these rules, and one draw needn't show every extreme that they name: `block_index`: each row names 3 different source blocks, and every block is named by some row.
All inputs are finite; a program needn't handle non-finite values.
Results may differ from a plain program's by a relative error of at most 0.004.
Values may be sent and summed in bfloat16 or wider, within the bound.
A program may use at most 64 MiB of HBM per device.

v0:
```python
import math

import jax
import jax.numpy as jnp
from jax import lax
from jax.sharding import PartitionSpec as P

NB = 4
BS = 64
BANDS = 3
NT = 512
RADIUS = 4
ITERS = 2
RECV = 384


step_size = 0.5
shrinkage = 0.05


def extended_2(value, sides, width):
    for axis, dim in sides:
        peers, length = (lax.axis_size(axis), value.shape[dim])
        up = [(i, (i + 1) % peers) for i in range(peers - 1)]
        down = [(j, i) for i, j in up]
        last = lax.slice_in_dim(value, length - width, length, axis=dim)
        leading = lax.slice_in_dim(value, 0, width, axis=dim)
        before = lax.ppermute(last, axis, up)
        after = lax.ppermute(leading, axis, down)
        value = jnp.concatenate([before, value, after], axis=dim)
    return value


def dft_table(freq_count):
    sample_ids = jnp.arange(NT, dtype=jnp.int32)
    bin_ids = jnp.arange(freq_count, dtype=jnp.int32) + 1
    phases = sample_ids[:, None] * bin_ids[None, :] % NT
    angles = phases.astype(jnp.float32) * (2.0 * math.pi / NT)
    stacked = jnp.stack([jnp.cos(angles), -jnp.sin(angles)], axis=-1)
    return stacked.reshape(NT, 2 * freq_count) / math.sqrt(NT)


def embed_complex(multiples):
    real_part = multiples[..., :BS]
    imag_part = multiples[..., BS:]
    upper_rows = jnp.concatenate([real_part, imag_part], axis=-1)
    lower_rows = jnp.concatenate([-imag_part, real_part], axis=-1)
    return jnp.concatenate([upper_rows, lower_rows], axis=-2)


def owner_layout(arrived, freq_count):
    shaped = arrived.reshape(freq_count, 2, NB, BS, arrived.shape[2])
    return shaped.transpose(0, 4, 2, 1, 3).reshape(freq_count, arrived.shape[2], NB, 2 * BS)


def trace_layout(backward, freq_count):
    shaped = backward.reshape(freq_count, backward.shape[1], NB, 2, BS)
    return shaped.transpose(0, 3, 2, 4, 1).reshape(2 * freq_count, NB * BS, backward.shape[1])


def smooth_along(extended, radius, rows_out, along):
    shares = 1.0 / (2.0 * radius.astype(jnp.float32) + 1.0)
    summed = None
    for offset in range(-RADIUS, RADIUS + 1):
        weight = jnp.where(abs(offset) <= radius, shares, 0.0)
        weight = weight[None, :, :]
        piece = lax.slice_in_dim(extended, RADIUS + offset, RADIUS + offset + rows_out, axis=along)
        term = weight * piece.astype(jnp.float32)
        summed = term if summed is None else summed + term
    return summed


def to_time(spectra, basis):
    return jnp.einsum("csr,tc->srt", spectra, basis, precision=lax.Precision.HIGH)


def on_device(start_field, recorded, multiples, block_index, radius):
    devices = lax.axis_size("freq")
    local_freq = recorded.shape[0]
    all_freq = local_freq * devices
    local_src = start_field.shape[0]
    basis = dft_table(all_freq)
    operator = embed_complex(multiples)
    field = start_field.astype(jnp.float32)
    residual = None
    for sweep in range(ITERS):
        spectra = jnp.einsum("srt,tc->csr", field, basis, precision=lax.Precision.HIGH).astype(
            jnp.bfloat16
        )
        arrived = lax.all_to_all(spectra, "freq", split_axis=0, concat_axis=1, tiled=True)
        owned = owner_layout(arrived, local_freq)
        predicted = []
        for out_block in range(NB):
            summed = None
            for band_id in range(BANDS):
                source = lax.dynamic_index_in_dim(
                    owned, block_index[out_block, band_id], axis=2, keepdims=False
                )
                term = jnp.einsum(
                    "frc,fcd->frd",
                    source,
                    operator[:, out_block, band_id],
                    preferred_element_type=jnp.float32,
                )
                summed = term if summed is None else summed + term
            predicted.append(summed)
        residual = recorded.astype(jnp.float32) - jnp.stack(predicted, axis=2)
        narrow = residual.astype(jnp.bfloat16)
        backward = jnp.zeros((local_freq, RECV, NB, 2 * BS), jnp.float32)
        for out_block in range(NB):
            for band_id in range(BANDS):
                contrib = jnp.einsum(
                    "frd,fcd->frc",
                    narrow[:, :, out_block],
                    operator[:, out_block, band_id],
                    preferred_element_type=jnp.float32,
                )
                target_block = block_index[out_block, band_id]
                current = lax.dynamic_index_in_dim(backward, target_block, axis=2, keepdims=False)
                backward = lax.dynamic_update_index_in_dim(
                    backward, current + contrib, target_block, 2
                )
        returned = trace_layout(backward.astype(jnp.bfloat16), local_freq)
        back_spec = lax.all_to_all(returned, "freq", split_axis=1, concat_axis=0, tiled=True)
        with_rim = extended_2(back_spec, (("freq", 1),), RADIUS)
        smoothed_spec = smooth_along(with_rim, radius, local_src, 1)
        smoothed = to_time(smoothed_spec, basis)
        update = field + step_size * smoothed
        field = jnp.sign(update) * jnp.maximum(jnp.abs(update) - shrinkage, 0.0)
    return (field, residual)


def solution(mesh):
    placed = (
        P(("grp", "freq"), None, None),
        P(("grp", "freq"), None, None, None),
        P(("grp", "freq"), None, None, None, None),
        P(),
        P(("grp", "freq"), None),
    )
    return jax.shard_map(
        on_device,
        mesh=mesh,
        in_specs=placed,
        out_specs=(P(("grp", "freq"), None, None), P(("grp", "freq"), None, None, None)),
        check_vma=False,
    )
```

profile of v0, /device:TPU:18, one launch (start us, length us, event | category | flops | bytes accessed | tf_op | source)
XLA Modules:
  0.0 152.4 jit_solution(5975691967619041598)
XLA Ops:
  0.6 0.2 fusion.155
  1.0 6.5 %convolution_convert_fusion.1 = bf16[32,16,384]{2,0,1:T(8,128)(2,1)S(1)} fusion(f32[512,32,1]{0,1,2:T(8,128)S(1)} %reshape.614, bf16[16,384,512]{2,1,0:T(8,128)(2,1)} %param.5), kind=kOutput, calls=%fused_computation.3 | convolution fusion | flops 604176384 | bytes 6750208 | tf_op jit(solution)/shard_map/srt,tc->csr/dot_general | solution.py:87
  7.5 0.9 copy.201
  8.3 6.2 %all-to-all-start = ((bf16[32,16,384]{2,1,0:T(8,128)(2,1)}), bf16[32,16,384]{2,1,0:T(8,128)(2,1)S(1)}, u32[]{:S(2)}, u32[]{:S(2)}) async-start(bf16[32,16,384]{2,1,0:T(8,128)(2,1)} %copy.201), calls=%async_computation | async-start | bytes 786432 | tf_op jit(solution)/shard_map/all_to_all | solution.py:90
  14.5 1.8 %fusion.159 = (s32[1,1]{1,0:T(1,128)}, s32[1,1]{1,0:T(1,128)}, s32[1,1]{1,0:T(1,128)}, s32[1,1]{1,0:T(1,128)}, s32[1,1]{1,0:T(1,128)}, /*index=5*/s32[1,1]{1,0:T...) fusion(s32[4,3]{1,0:T(4,128)} %param.8), kind=kLoop, calls=%fused_computation.291 | loop fusion | bytes 96 | tf_op jit(solution)/shard_map/slice | solution.py:97
  39.4 1.1 slice_negate_fusion
  40.6 1.1 maximum_maximum_fusion
  41.8 0.2 fusion.87
  42.0 0.2 fusion.91
  42.2 0.2 fusion.95
  42.5 0.2 fusion.99
  42.7 0.2 convolution_add_fusion.31
  42.9 0.2 fusion.3
  43.1 0.2 convolution_add_fusion.33
  43.3 0.2 fusion.2
  43.6 0.2 convolution_add_fusion.35
  43.8 0.2 fusion.1
  44.0 0.2 convolution_add_fusion.37
  44.2 0.2 fusion
  45.3 0.2 fusion.9
  45.5 0.2 fusion.11
  45.8 0.2 fusion.13
  46.0 0.2 fusion.15
  46.2 0.2 fusion.17
  47.5 0.4 copy.217
  47.9 16.9 %all_to_all.66 = bf16[2,256,384]{2,0,1:T(2,128)(2,1)S(1)} all-to-all(bf16[2,256,384]{2,0,1:T(2,128)(2,1)S(1)} %copy.217), channel_id=1, replica_groups=mesh['grp'=2,'freq'=16] {'freq'}, dimensions={1} | all-to-all | bytes 786432 | tf_op jit(solution)/shard_map/all_to_all | solution.py:124
  64.9 1.9 %collective-permute-start = (bf16[32,4,384]{2,1,0:T(4,128)(2,1)S(1)}, bf16[32,4,384]{2,1,0:T(4,128)(2,1)S(1)}, u32[]{:S(2)}, u32[]{:S(2)}) collective-permute-start(bf16[32,4,384]{2,1,0:T(4,128)(2,1)S(1)} %get-tuple-element.20), channel_id=1, source_target_pairs={{0,1},{1,2},{2,3},{3,4},{4,5},{5,6},{6,7},{7,8},{8,9},{9,10},{10,1... | collective-permute-start | bytes 294920 | tf_op jit(solution)/shard_map/ppermute | solution.py:28
  66.9 4.7 %collective-permute-start.1 = (bf16[32,4,384]{2,1,0:T(4,128)(2,1)S(1)}, bf16[32,4,384]{2,1,0:T(4,128)(2,1)S(1)}, u32[]{:S(2)}, u32[]{:S(2)}) collective-permute-start(bf16[32,4,384]{2,1,0:T(4,128)(2,1)S(1)} %get-tuple-element.21), channel_id=1, source_target_pairs={{1,0},{2,1},{3,2},{4,3},{5,4},{6,5},{7,6},{8,7},{9,8},{10,9},{11,1... | collective-permute-start | bytes 294920 | tf_op jit(solution)/shard_map/ppermute | solution.py:29
  71.8 1.8 %collective-permute-done.1 = bf16[32,4,384]{2,1,0:T(4,128)(2,1)S(1)} collective-permute-done((bf16[32,4,384]{2,1,0:T(4,128)(2,1)S(1)}, bf16[32,4,384]{2,1,0:T(4,128)(2,1)S(1)}, u32[]{:S(2)}, u32[]{:S(2)}) %collective-permute-start.1) | collective-permute-done | bytes 98336 | tf_op jit(solution)/shard_map/ppermute | solution.py:29
  73.6 1.2 multiply_add_fusion.1
  74.8 10.3 %maximum_multiply_fusion.1 = f32[16,384,512]{2,1,0:T(8,128)S(1)} fusion(bf16[16,384,512]{2,1,0:T(8,128)(2,1)S(1)} %bitcast.415, f32[512,32,1]{0,1,2:T(8,128)S(1)} %reshape.614, f32[32,16,384]{2,1,0:T(8,128)S(1)} %multiply_add_fusion.1), kind=kOutput, calls=%fused_computation.1 | convolution fusion | flops 629145600 | bytes 19726336 | tf_op jit(solution)/shard_map/csr,tc->srt/dot_general | solution.py:74
  85.2 6.1 %convolution_convert_fusion = bf16[32,16,384]{2,0,1:T(8,128)(2,1)S(1)} fusion(f32[512,32,1]{0,1,2:T(8,128)S(1)} %reshape.614, f32[16,384,512]{2,1,0:T(8,128)S(1)} %maximum_multiply_fusion.1), kind=kOutput, calls=%fused_computation.2 | convolution fusion | flops 604176384 | bytes 13041664 | tf_op jit(solution)/shard_map/srt,tc->csr/dot_general | solution.py:87
  91.4 16.3 %all_to_all.67 = bf16[32,16,384]{2,1,0:T(8,128)(2,1)S(1)} all-to-all(bf16[32,16,384]{2,1,0:T(8,128)(2,1)S(1)} %copy.221), channel_id=1, replica_groups=mesh['grp'=2,'freq'=16] {'freq'}, dimensions={0} | all-to-all | bytes 786432 | tf_op jit(solution)/shard_map/all_to_all | solution.py:90
  107.9 0.2 fusion.71
  108.1 0.2 fusion.75
  108.3 0.2 fusion.79
  108.5 0.2 fusion.83
  108.7 0.2 convolution_add_fusion.12
  109.0 0.2 fusion.29
  109.2 0.2 convolution_add_fusion.14
  109.4 0.2 fusion.28
  109.6 0.2 convolution_add_fusion.16
  109.9 0.2 fusion.27
  110.1 0.2 convolution_add_fusion.18
  110.3 0.2 fusion.26
  110.9 0.2 fusion.31
  111.2 0.2 fusion.33
  111.4 0.2 fusion.35
  111.6 0.2 fusion.37
  111.9 0.2 fusion.39
  112.1 0.2 fusion.41
  112.3 0.2 fusion.43
  112.5 0.2 fusion.45
  112.8 0.2 fusion.47
  113.0 0.2 fusion.49
  113.2 0.2 fusion.51
  113.5 0.4 copy.237
  113.9 15.4 %all_to_all.68 = bf16[2,256,384]{2,0,1:T(2,128)(2,1)S(1)} all-to-all(bf16[2,256,384]{2,0,1:T(2,128)(2,1)S(1)} %copy.237), channel_id=1, replica_groups=mesh['grp'=2,'freq'=16] {'freq'}, dimensions={1} | all-to-all | bytes 786432 | tf_op jit(solution)/shard_map/all_to_all | solution.py:124
  129.5 1.9 %collective-permute-start.2 = (bf16[32,4,384]{2,1,0:T(4,128)(2,1)S(1)}, bf16[32,4,384]{2,1,0:T(4,128)(2,1)S(1)}, u32[]{:S(2)}, u32[]{:S(2)}) collective-permute-start(bf16[32,4,384]{2,1,0:T(4,128)(2,1)S(1)} %get-tuple-element.18), channel_id=1, source_target_pairs={{0,1},{1,2},{2,3},{3,4},{4,5},{5,6},{6,7},{7,8},{8,9},{9,10},{10,1... | collective-permute-start | bytes 294920 | tf_op jit(solution)/shard_map/ppermute | solution.py:28
  131.5 4.8 %collective-permute-start.3 = (bf16[32,4,384]{2,1,0:T(4,128)(2,1)S(1)}, bf16[32,4,384]{2,1,0:T(4,128)(2,1)S(1)}, u32[]{:S(2)}, u32[]{:S(2)}) collective-permute-start(bf16[32,4,384]{2,1,0:T(4,128)(2,1)S(1)} %get-tuple-element.19), channel_id=1, source_target_pairs={{1,0},{2,1},{3,2},{4,3},{5,4},{6,5},{7,6},{8,7},{9,8},{10,9},{11,1... | collective-permute-start | bytes 294920 | tf_op jit(solution)/shard_map/ppermute | solution.py:29
  136.3 1.4 copy.241
  137.7 0.5 collective-permute-done.3
  138.2 1.2 multiply_add_fusion
  139.4 12.9 %maximum_multiply_fusion = f32[16,384,512]{2,1,0:T(8,128)} fusion(f32[16,384,512]{2,1,0:T(8,128)S(1)} %maximum_multiply_fusion.1, f32[512,32,1]{0,1,2:T(8,128)S(1)} %reshape.614, f32[32,16,384]{2,1,0:T(8,128)S(1)} %multiply_add_fusion), kind=kOutput, calls=%fused_computation | convolution fusion | flops 625999872 | bytes 26017792 | tf_op jit(solution)/shard_map/csr,tc->srt/dot_general | solution.py:74
  (66 shorter events, 3.4 us)
Async XLA Ops:
  0.6 43.8 %copy-start = (bf16[1,384,4,128]{3,2,1,0:T(4,128)(2,1)S(1)}, bf16[1,384,4,128]{3,2,1,0:T(4,128)(2,1)}, u32[]{:S(2)}) copy-start(bf16[1,384,4,128]{3,2,1,0:T(4,128)(2,1)} %param.6) | copy-start | bytes 1179652
  8.3 33.3 %all-to-all-start = ((bf16[32,16,384]{2,1,0:T(8,128)(2,1)}), bf16[32,16,384]{2,1,0:T(8,128)(2,1)S(1)}, u32[]{:S(2)}, u32[]{:S(2)}) async-start(bf16[32,16,384]{2,1,0:T(8,128)(2,1)} %copy.201), calls=%async_computation | async-start | bytes 786432 | tf_op jit(solution)/shard_map/all_to_all | solution.py:90
  41.7 29.9 %copy-start.1 = (s32[16,384]{1,0:T(8,128)S(1)}, s32[16,384]{1,0:T(8,128)}, u32[]{:S(2)}) copy-start(s32[16,384]{1,0:T(8,128)} %param.9) | copy-start | bytes 73732
  42.0 32.8 %slice-start = ((s8[6291456]{0:T(1024)(128)(4,1)}), s8[4194304]{0:T(1024)(128)(4,1)S(1)}, s32[]{:S(2)}) async-start(s8[6291456]{0:T(1024)(128)(4,1)} %bitcast.414), calls=%async_computation.4 | async-start | bytes 8388608
  46.0 28.9 %slice-start.1 = ((s8[6291456]{0:T(1024)(128)(4,1)}), s8[2097152]{0:T(1024)(128)(4,1)S(1)}, s32[]{:S(2)}) async-start(s8[6291456]{0:T(1024)(128)(4,1)} %bitcast.414), calls=%async_computation.5 | async-start | bytes 4194304
  64.9 6.9 %collective-permute-start = (bf16[32,4,384]{2,1,0:T(4,128)(2,1)S(1)}, bf16[32,4,384]{2,1,0:T(4,128)(2,1)S(1)}, u32[]{:S(2)}, u32[]{:S(2)}) collective-permute-start(bf16[32,4,384]{2,1,0:T(4,128)(2,1)S(1)} %get-tuple-element.20), channel_id=1, source_target_pairs={{0,1},{1,2},{2,3},{3,4},{4,5},{5,6},{6,7},{7,8},{8,9},{9,10},{10,1... | collective-permute-start | bytes 294920 | tf_op jit(solution)/shard_map/ppermute | solution.py:28
  66.9 6.7 %collective-permute-start.1 = (bf16[32,4,384]{2,1,0:T(4,128)(2,1)S(1)}, bf16[32,4,384]{2,1,0:T(4,128)(2,1)S(1)}, u32[]{:S(2)}, u32[]{:S(2)}) collective-permute-start(bf16[32,4,384]{2,1,0:T(4,128)(2,1)S(1)} %get-tuple-element.21), channel_id=1, source_target_pairs={{1,0},{2,1},{3,2},{4,3},{5,4},{6,5},{7,6},{8,7},{9,8},{10,9},{11,1... | collective-permute-start | bytes 294920 | tf_op jit(solution)/shard_map/ppermute | solution.py:29
  129.5 8.1 %collective-permute-start.2 = (bf16[32,4,384]{2,1,0:T(4,128)(2,1)S(1)}, bf16[32,4,384]{2,1,0:T(4,128)(2,1)S(1)}, u32[]{:S(2)}, u32[]{:S(2)}) collective-permute-start(bf16[32,4,384]{2,1,0:T(4,128)(2,1)S(1)} %get-tuple-element.18), channel_id=1, source_target_pairs={{0,1},{1,2},{2,3},{3,4},{4,5},{5,6},{6,7},{7,8},{8,9},{9,10},{10,1... | collective-permute-start | bytes 294920 | tf_op jit(solution)/shard_map/ppermute | solution.py:28
  131.5 6.7 %collective-permute-start.3 = (bf16[32,4,384]{2,1,0:T(4,128)(2,1)S(1)}, bf16[32,4,384]{2,1,0:T(4,128)(2,1)S(1)}, u32[]{:S(2)}, u32[]{:S(2)}) collective-permute-start(bf16[32,4,384]{2,1,0:T(4,128)(2,1)S(1)} %get-tuple-element.19), channel_id=1, source_target_pairs={{1,0},{2,1},{3,2},{4,3},{5,4},{6,5},{7,6},{8,7},{9,8},{10,9},{11,1... | collective-permute-start | bytes 294920 | tf_op jit(solution)/shard_map/ppermute | solution.py:29
where the time goes:
time: 155 us; the launch traced here: 152 us
  blocking collectives  48.6 us (31%)
  matrix products  45.6 us (29%)
  between operations  24.6 us (16%)
  starting transfers between devices  19.5 us (13%)
  local copies, waits for them, and re-layouts  6.33 us (4%)
  other arithmetic  5.18 us (3%)
  waiting for transfers between devices  2.52 us (2%)
    all_to_all x2, blocking collectives, on_device(): lax.all_to_all(returned, 'freq', split_axis=1, concat_axis=0, tiled=True)  32.3 us
    dot_general x2, matrix products, to_time(): jnp.einsum('csr,tc->srt', spectra, basis, precision=lax.Precision.HIGH)  23.3 us
    all_to_all x1, blocking collectives, on_device(): lax.all_to_all(spectra, 'freq', split_axis=0, concat_axis=1, tiled=True)  16.3 us
    dot_general x2, matrix products, on_device(): jnp.einsum('srt,tc->csr', field, basis, precision=lax.Precision.HIGH)  12.6 us
    ppermute x2, starting transfers between devices, extended_2(): after = lax.ppermute(leading, axis, down)  9.52 us
    all_to_all x1, starting transfers between devices, on_device(): lax.all_to_all(spectra, 'freq', split_axis=0, concat_axis=1, tiled=True)  6.18 us
    dot_general x24, matrix products, on_device(): jnp.einsum('frc,fcd->frd', source, operator[:, out_block, band_id], prefe...  5.18 us
    dot_general x24, matrix products, on_device(): jnp.einsum('frd,fcd->frc', narrow[:, :, out_block], operator[:, out_block...  4.56 us
  transfers between devices with their start and end apart: 5, of which 3 were waited for; matrix products, arithmetic and copies ran while one was open for 4% of the time, Pallas kernels for 0%

commit v1 on v0

v1 whole, which is shorter than its diff:
```python
import functools
import math

import jax
import jax.numpy as jnp
import numpy as np
from jax import lax
from jax.experimental import pallas as pl
from jax.experimental.pallas import tpu as pltpu
from jax.sharding import PartitionSpec as P

NB = 4
BS = 64
BANDS = 3
RADIUS = 4

step_size = 0.5
shrinkage = 0.05

BF16 = jnp.bfloat16
F32 = jnp.float32


def dft_table(freq_count, samples):
    phases = (np.arange(samples)[:, None] * (np.arange(freq_count) + 1)[None, :]) % samples
    angles = phases.astype(np.float64) * (2.0 * math.pi / samples)
    stacked = np.stack([np.cos(angles), -np.sin(angles)], axis=-1)
    return (stacked.reshape(samples, 2 * freq_count) / math.sqrt(samples)).astype(np.float32)


def halves(table):
    high = jnp.asarray(table).astype(BF16)
    low = (jnp.asarray(table) - high.astype(F32)).astype(BF16)
    return high, low


def embed_complex(multiples):
    real_part = multiples[..., :BS]
    imag_part = multiples[..., BS:]
    upper_rows = jnp.concatenate([real_part, imag_part], axis=-1)
    lower_rows = jnp.concatenate([-imag_part, real_part], axis=-1)
    return jnp.stack([upper_rows, lower_rows], axis=-3)


def dense_operators(multiples, block_index, devices, local_src):
    local_freq = multiples.shape[0]
    op = embed_complex(multiples)
    dense = None
    blocks = jnp.arange(NB, dtype=block_index.dtype)
    for band in range(BANDS):
        hit = block_index[:, band][None, :] == blocks[:, None]
        term = jnp.where(hit[None, :, None, None, :, None], op[:, :, band].transpose(0, 2, 3, 1, 4)[:, None], 0)
        dense = term if dense is None else dense + term
    sources = NB * BS
    by_part = dense.transpose(0, 2, 1, 3, 4, 5).reshape(local_freq, 2, sources, NB * 2 * BS)
    padded = jnp.pad(by_part, ((0, 0), (0, 0), (RADIUS, RADIUS), (0, 0)))
    inner = by_part.reshape(local_freq, 2, devices, local_src, NB * 2 * BS).transpose(0, 2, 1, 3, 4)
    reach = local_src + 2 * RADIUS
    outer = jnp.stack([padded[:, :, d * local_src : d * local_src + reach] for d in range(devices)], axis=1)
    columns = NB * 2 * BS
    return (
        inner.reshape(local_freq, devices * 2 * local_src, columns),
        outer.reshape(local_freq, devices * 2 * reach, columns),
    )


def soft(update):
    return update - jnp.clip(update, -shrinkage, shrinkage)


def nt_dot(a, b):
    return lax.dot_general(a, b, (((1,), (1,)), ((), ())), preferred_element_type=F32)


def tn_dot(a, b):
    return lax.dot_general(a, b, (((0,), (0,)), ((), ())), preferred_element_type=F32)


def sweeps_kernel(
    devices, chunks, width,
    start_hbm, recorded_ref, inner_ref, outer_ref, radius_ref, analysis_ref, synthesis_ref,
    first_ref, second_ref, residual_ref,
    field, wide, reach_wide, out_slabs, in_slabs, back_slabs, edge_slabs,
    load_sem, send_sem, recv_sem,
):
    me = lax.axis_index("freq")
    local_src = start_hbm.shape[0]
    local_freq = recorded_ref.shape[0]
    rows = analysis_ref.shape[0] // 2
    reach = local_src + 2 * RADIUS

    def load(c):
        return pltpu.make_async_copy(start_hbm.at[:, pl.ds(c * width, width), :], field.at[c], load_sem.at[c])

    for c in range(chunks):
        load(c).start()
    barrier = pltpu.get_barrier_semaphore()
    for shift in range(1, devices):
        pl.semaphore_signal(
            barrier, inc=1, device_id={"freq": lax.rem(me + shift, devices)}, device_id_type=pl.DeviceIdType.MESH
        )

    def exchange(phase, c, sources, targets):
        slot = phase * chunks + c

        def send(step, carry):
            peer = lax.rem(me + step, devices)
            pltpu.make_async_remote_copy(
                src_ref=sources.at[(phase // 2) * chunks + c, peer],
                dst_ref=targets.at[(phase // 2) * chunks + c, me],
                send_sem=send_sem.at[slot],
                recv_sem=recv_sem.at[slot],
                device_id={"freq": peer},
                device_id_type=pl.DeviceIdType.MESH,
            ).start()
            return carry

        lax.fori_loop(1, devices, send, 0)
        targets[(phase // 2) * chunks + c, me] = sources[(phase // 2) * chunks + c, me]

    def await_all(phase, c, refs, sems):
        whole = refs.at[(phase // 2) * chunks + c, pl.ds(0, devices - 1)]
        pltpu.make_async_copy(whole, whole, sems.at[phase * chunks + c]).wait()

    def analyse(s, samples):
        both = nt_dot(analysis_ref[...], samples)
        wide[pl.ds(s, rows, stride=local_src), :] = both[:rows] + both[rows:]

    def ship(sweep, c):
        slabs = wide[...].reshape(devices, local_freq * 2 * local_src, width)
        out_slabs[sweep * chunks + c] = slabs.astype(BF16)
        if sweep == 0 and c == 0:
            pl.semaphore_wait(barrier, devices - 1)
        exchange(2 * sweep, c, out_slabs, in_slabs)

    def own(sweep, c):
        await_all(2 * sweep, c, in_slabs, recv_sem)
        arrived = in_slabs[sweep * chunks + c].astype(F32)
        backs = []
        for f in range(local_freq):
            part = arrived[:, f * 2 * local_src : (f + 1) * 2 * local_src]
            owned = part.reshape(devices * 2 * local_src, width).T.astype(BF16)
            predicted = jnp.dot(owned, inner_ref[f], preferred_element_type=F32)
            residual = recorded_ref[f, pl.ds(c * width, width), :].astype(F32) - predicted
            if sweep == 1:
                residual_ref[f, pl.ds(c * width, width), :] = residual
            back = nt_dot(outer_ref[f], residual.astype(BF16))
            backs.append(back.reshape(devices, 2 * reach, width))
        back = backs[0] if local_freq == 1 else jnp.concatenate(backs, axis=1)
        back_slabs[sweep * chunks + c] = back.astype(BF16)
        exchange(2 * sweep + 1, c, back_slabs, edge_slabs)

    def trace_side(sweep, c, stack_ref):
        await_all(2 * sweep + 1, c, edge_slabs, recv_sem)
        reach_wide[...] = edge_slabs[sweep * chunks + c].astype(F32).reshape(rows * reach, width)

        def source(s, carry):
            span = radius_ref[s, :, pl.ds(c * width, width)]
            tap = lambda offset: reach_wide[pl.ds(s + RADIUS + offset, rows, stride=reach), :]
            box = tap(0)
            smoothed = box
            for offset in range(1, RADIUS + 1):
                box = box + (tap(offset) + tap(-offset))
                smoothed = jnp.where(span >= offset, box, smoothed)
            smoothed = smoothed * (1.0 / (2.0 * span.astype(F32) + 1.0))
            high = smoothed.astype(BF16)
            low = (smoothed - high.astype(F32)).astype(BF16)
            stack = jnp.concatenate([high, low, high], axis=0)
            stack_ref[s, :, pl.ds(c * width, width)] = stack
            if sweep == 0:
                update = field[c, s].astype(F32) + tn_dot(stack, synthesis_ref[...])
                analyse(s, soft(update).astype(BF16))
            return carry

        lax.fori_loop(0, local_src, source, 0, unroll=2)
        if sweep == 0:
            ship(1, c)

    for c in range(chunks):
        load(c).wait()

        def source(s, carry):
            analyse(s, field[c, s])
            return carry

        lax.fori_loop(0, local_src, source, 0, unroll=4)
        ship(0, c)
    for c in range(chunks):
        own(0, c)
    for c in range(chunks):
        trace_side(0, c, first_ref)
    for c in range(chunks):
        own(1, c)
    for c in range(chunks):
        trace_side(1, c, second_ref)
    for phase in range(4):
        for c in range(chunks):
            await_all(phase, c, back_slabs if phase % 2 else out_slabs, send_sem)


def finish_kernel(start_ref, first_ref, second_ref, synthesis_ref, field_ref):
    table = synthesis_ref[...]
    once = soft(start_ref[0].astype(F32) + tn_dot(first_ref[0], table))
    field_ref[0] = soft(once + tn_dot(second_ref[0], table))


def on_device(devices, start_field, recorded, multiples, block_index, radius):
    local_src, receivers, samples = start_field.shape
    local_freq = recorded.shape[0]
    columns = NB * 2 * BS
    rows = 2 * local_freq * devices
    width = 128
    chunks = receivers // width
    reach = local_src + 2 * RADIUS
    table = dft_table(local_freq * devices, samples)
    analysis = jnp.concatenate(halves(table.T), axis=0)
    high, low = halves(step_size * table.T)
    synthesis = jnp.concatenate([high, high, low], axis=0)
    inner, outer = dense_operators(multiples, block_index, devices, local_src)
    vmem = pl.BlockSpec(memory_space=pltpu.VMEM)
    slab = lambda height: pltpu.VMEM((2 * chunks, devices, local_freq * 2 * height, width), BF16)
    stack_shape = jax.ShapeDtypeStruct((local_src, 3 * rows, receivers), BF16)
    first, second, residual = pl.pallas_call(
        functools.partial(sweeps_kernel, devices, chunks, width),
        out_shape=(stack_shape, stack_shape, jax.ShapeDtypeStruct((local_freq, receivers, columns), F32)),
        in_specs=[pl.BlockSpec(memory_space=pl.ANY)] + [vmem] * 6,
        out_specs=(vmem, vmem, vmem),
        scratch_shapes=[
            pltpu.VMEM((chunks, local_src, width, samples), BF16),
            pltpu.VMEM((rows * local_src, width), F32),
            pltpu.VMEM((rows * reach, width), F32),
            slab(local_src),
            slab(local_src),
            slab(reach),
            slab(reach),
            pltpu.SemaphoreType.DMA((chunks,)),
            pltpu.SemaphoreType.DMA((4 * chunks,)),
            pltpu.SemaphoreType.DMA((4 * chunks,)),
        ],
        compiler_params=pltpu.CompilerParams(
            collective_id=0, has_side_effects=True, vmem_limit_bytes=48 << 20
        ),
    )(start_field, recorded.reshape(local_freq, receivers, columns), inner, outer,
      radius.reshape(local_src, 1, receivers), analysis, synthesis)
    field = pl.pallas_call(
        finish_kernel,
        grid=(local_src,),
        out_shape=jax.ShapeDtypeStruct(start_field.shape, F32),
        in_specs=[
            pl.BlockSpec((1, receivers, samples), lambda s: (s, 0, 0)),
            pl.BlockSpec((1, 3 * rows, receivers), lambda s: (s, 0, 0)),
            pl.BlockSpec((1, 3 * rows, receivers), lambda s: (s, 0, 0)),
            pl.BlockSpec((3 * rows, samples), lambda s: (0, 0)),
        ],
        out_specs=pl.BlockSpec((1, receivers, samples), lambda s: (s, 0, 0)),
    )(start_field, first, second, synthesis)
    return field, residual.reshape(recorded.shape)


def solution(mesh):
    placed = (
        P(("grp", "freq"), None, None),
        P(("grp", "freq"), None, None, None),
        P(("grp", "freq"), None, None, None, None),
        P(),
        P(("grp", "freq"), None),
    )
    return jax.shard_map(
        functools.partial(on_device, mesh.shape["freq"]),
        mesh=mesh,
        in_specs=placed,
        out_specs=(P(("grp", "freq"), None, None), P(("grp", "freq"), None, None, None)),
        check_vma=False,
    )
```

time: 155 us -> 82.2 us (0.53)
  the two profiles are of different devices: /device:TPU:18 before, /device:TPU:25 now
where the time goes in v1:
time: 82.2 us; the launch traced here: 81.6 us
  Pallas kernels  70.9 us (86%)
  local copies, waits for them, and re-layouts  7.13 us (9%)
  other arithmetic  2.66 us (3%)
  between operations  0.89 us (1%)
    pallas_call x1, Pallas kernels, on_device(): pl.pallas_call(functools.partial(sweeps_kernel, devices, chunks, width),...  55.4 us
    pallas_call x1, Pallas kernels, on_device(): pl.pallas_call(finish_kernel, grid=(local_src,), out_shape=jax.ShapeDtype...  15.5 us
    unnamed x23, local copies, waits for them, and re-layouts  2.31 us

profile of v1, /device:TPU:25, one launch (start us, length us, event | category | flops | bytes accessed | tf_op | source)
XLA Modules:
  0.0 81.6 jit_solution(495506914174216751)
XLA Ops:
  0.6 0.0 copy-start.2
  0.6 0.0 copy-start.3
  0.7 1.0 %slice_reduce_fusion.2 = (s32[4]{0:T(128)S(1)}, s32[4]{0:T(128)S(1)}, s32[4]{0:T(128)S(1)}) fusion(s32[4,3]{1,0:T(4,128)} %param.10), kind=kLoop, calls=%fused_computation.52 | loop fusion | bytes 96 | tf_op jit(solution)/shard_map/slice | solution.py:51
  1.7 0.8 reshape.130.radius_ref
  2.4 1.1 %reshape.126.recorded_ref = bf16[1,384,512]{2,1,0:T(8,128)(2,1)S(1)} reshape(bf16[1,384,4,128]{3,2,1,0:T(4,128)(2,1)} %param.8) | data formatting | bytes 786432 | tf_op jit(solution)/shard_map/reshape | solution.py:243
  3.6 1.1 %slice_negate_fusion = (bf16[1,4,3,64,64]{4,3,2,1,0:T(8,128)(2,1)S(1)}, bf16[1,4,3,64,64]{4,3,2,1,0:T(8,128)(2,1)S(1)}) fusion(bf16[1,4,3,64,128]{4,3,2,1,0:T(8,128)(2,1)} %param.9), kind=kLoop, calls=%fused_computation.8 | loop fusion | flops 49152 | bytes 393216 | tf_op jit(solution)/shard_map/neg | solution.py:41
  4.8 0.1 maximum_bitcast_fusion
  4.9 0.9 %fusion.3 = (bf16[2,64,4,128]{3,1,2,0:T(8,128)(2,1)S(1)}, bf16[2,64,4,128]{3,1,2,0:T(8,128)(2,1)S(1)}, bf16[2,64,4,128]{3,1,2,0:T(8,128)(2,1)S(1)}) fusion(bf16[1,4,3,1,64,128]{5,4,2,1,3,0:T(8,128)(2,1)} %bitcast.93, bf16[1,4,3,1,64,128]{5,4,2,1,3,0:T(8,128)(2,1)S(1)} %maximum_bitcast_fusion), kind=kLoop, calls=%fused_computation.12 | loop fusion | flops 196608 | bytes 786432 | tf_op jit(solution)/shard_map/jit(_where)/broadcast_in_dim | solution.py:52
  5.8 0.1 copy.12
  6.0 0.1 copy.14
  6.1 0.1 copy.13
  6.2 0.4 add_bitcast_fusion
  6.6 0.2 reshape.128
  6.8 0.2 reshape_reshape.3
  7.5 0.0 copy-done.2
  7.5 0.0 copy-done.3
  7.5 55.4 %shard_map.86 = (bf16[16,96,384]{2,1,0:T(8,128)(2,1)S(1)}, bf16[16,96,384]{2,1,0:T(8,128)(2,1)S(1)}, f32[1,384,512]{2,1,0:T(8,128)S(1)}) custom-call(bf16[16,384,512]{2,1,0:T(8,128)(2,1)} %start_ref.1, bf16[1,384,512]{2,1,0:T(8,128)(2,1)S(1)} %reshape.126.recorded_ref, bf16[1,512,512]{2,1,0:T(8,128)(2,1)S(1)} %bitcast.90, bf16[1,768,512]{2,1,0:T(8,128)(2,1)S(1)} %bitcast.91, ...), custom_call_target="tpu_custom_call" | custom-call | tf_op jit(solution)/shard_map/pallas_call | solution.py:223
  62.8 0.0 copy-start
  62.9 1.0 %copy-done = bf16[16,96,384]{2,1,0:T(8,128)(2,1)} copy-done((bf16[16,96,384]{2,1,0:T(8,128)(2,1)}, bf16[16,96,384]{2,1,0:T(8,128)(2,1)S(1)}, u32[]{:S(2)}) %copy-start) | copy-done | bytes 1179672
  63.9 0.0 copy-start.1
  63.9 1.0 %copy-done.1 = bf16[16,96,384]{2,1,0:T(8,128)(2,1)} copy-done((bf16[16,96,384]{2,1,0:T(8,128)(2,1)}, bf16[16,96,384]{2,1,0:T(8,128)(2,1)S(1)}, u32[]{:S(2)}) %copy-start.1) | copy-done | bytes 1179672
  64.9 1.1 %reshape.131 = f32[1,384,4,128]{3,2,1,0:T(4,128)} reshape(f32[1,384,512]{2,1,0:T(8,128)S(1)} %get-tuple-element.7) | data formatting | bytes 1572864 | tf_op jit(solution)/shard_map/reshape | solution.py:257
  66.0 15.5 %shard_map.87 = f32[16,384,512]{2,1,0:T(8,128)} custom-call(bf16[16,384,512]{2,1,0:T(8,128)(2,1)} %start_ref.1, bf16[16,96,384]{2,1,0:T(8,128)(2,1)} %copy-done, bf16[16,96,384]{2,1,0:T(8,128)(2,1)} %copy-done.1, bf16[96,512]{1,0:T(8,128)(2,1)} %constant.24.synthesis_ref), custom_call_target="tpu_custom_call" | custom-call | tf_op jit(solution)/shard_map/pallas_call | solution.py:245
  (19 shorter events, 0.3 us)
Async XLA Ops:
  0.6 6.8 %copy-start.2 = (bf16[96,512]{1,0:T(8,128)(2,1)S(1)}, bf16[96,512]{1,0:T(8,128)(2,1)}, u32[]{:S(2)}) copy-start(bf16[96,512]{1,0:T(8,128)(2,1)} %constant.24.synthesis_ref) | copy-start | bytes 294916
  0.6 6.8 %copy-start.3 = (bf16[64,512]{1,0:T(8,128)(2,1)S(1)}, bf16[64,512]{1,0:T(8,128)(2,1)}, u32[]{:S(2)}) copy-start(bf16[64,512]{1,0:T(8,128)(2,1)} %constant.19.analysis_ref) | copy-start | bytes 196612
  62.8 1.0 %copy-start = (bf16[16,96,384]{2,1,0:T(8,128)(2,1)}, bf16[16,96,384]{2,1,0:T(8,128)(2,1)S(1)}, u32[]{:S(2)}) copy-start(bf16[16,96,384]{2,1,0:T(8,128)(2,1)S(1)} %get-tuple-element.5.first_ref) | copy-start | bytes 3538948
  63.9 1.0 %copy-start.1 = (bf16[16,96,384]{2,1,0:T(8,128)(2,1)}, bf16[16,96,384]{2,1,0:T(8,128)(2,1)S(1)}, u32[]{:S(2)}) copy-start(bf16[16,96,384]{2,1,0:T(8,128)(2,1)S(1)} %get-tuple-element.6.second_ref) | copy-start | bytes 3538948

commit v2 on v1

v2 whole, which is shorter than its diff:
```python
import functools
import math

import jax
import jax.numpy as jnp
import numpy as np
from jax import lax
from jax.experimental import pallas as pl
from jax.experimental.pallas import tpu as pltpu
from jax.sharding import PartitionSpec as P

NB = 4
BS = 64
BANDS = 3
RADIUS = 4

step_size = 0.5
shrinkage = 0.05

BF16 = jnp.bfloat16
F32 = jnp.float32


def dft_table(freq_count, samples):
    phases = (np.arange(samples)[:, None] * (np.arange(freq_count) + 1)[None, :]) % samples
    angles = phases.astype(np.float64) * (2.0 * math.pi / samples)
    stacked = np.stack([np.cos(angles), -np.sin(angles)], axis=-1)
    return (stacked.reshape(samples, 2 * freq_count) / math.sqrt(samples)).astype(np.float32)


def halves(table):
    high = jnp.asarray(table).astype(BF16)
    low = (jnp.asarray(table) - high.astype(F32)).astype(BF16)
    return high, low


def soft(update):
    return update - jnp.clip(update, -shrinkage, shrinkage)


def nt_dot(a, b):
    return lax.dot_general(a, b, (((1,), (1,)), ((), ())), preferred_element_type=F32)


def tn_dot(a, b):
    return lax.dot_general(a, b, (((0,), (0,)), ((), ())), preferred_element_type=F32)


def build_operator(block_ref, multiples_ref, inner, local_src):
    parts = BS // local_src
    for f in range(multiples_ref.shape[0]):
        for j in range(NB):
            terms = [multiples_ref[f, j, b].astype(F32) for b in range(BANDS)]
            for m in range(NB):
                block = None
                for b in range(BANDS):
                    term = terms[b] * jnp.where(block_ref[j, b] == m, 1.0, 0.0)
                    block = term if block is None else block + term
                turned = jnp.concatenate([-block[:, BS:], block[:, :BS]], axis=1)
                for q in range(parts):
                    for c, half in enumerate((block, turned)):
                        row = ((m * parts + q) * 2 + c) * local_src
                        piece = half[q * local_src : (q + 1) * local_src]
                        inner[f, row : row + local_src, j * 2 * BS : (j + 1) * 2 * BS] = piece.astype(BF16)


def sweeps_kernel(
    devices, chunks, width,
    block_ref, start_hbm, recorded_ref, multiples_ref, radius_ref, analysis_ref, synthesis_ref,
    field_ref, last_ref, residual_ref,
    field, wide, flat, near, spans, given, inner, out_slabs, in_slabs, back_slabs, edge_slabs, rim_out, rim_in,
    load_sem, send_sem, recv_sem, rim_send, rim_recv,
):
    me = lax.axis_index("freq")
    local_src = start_hbm.shape[0]
    local_freq = multiples_ref.shape[0]
    rows = analysis_ref.shape[0] // 2
    block_cols = 2 * BS

    def load(c):
        return pltpu.make_async_copy(start_hbm.at[:, pl.ds(c * width, width), :], field.at[c], load_sem.at[c])

    for c in range(chunks):
        load(c).start()
    barrier = pltpu.get_barrier_semaphore()
    for shift in range(1, devices):
        pl.semaphore_signal(
            barrier, inc=1, device_id={"freq": lax.rem(me + shift, devices)}, device_id_type=pl.DeviceIdType.MESH
        )

    def exchange(phase, c, sources, targets):
        slot = phase * chunks + c
        place = (phase // 2) * chunks + c

        def send(step, carry):
            peer = lax.rem(me + step, devices)
            pltpu.make_async_remote_copy(
                src_ref=sources.at[place, peer],
                dst_ref=targets.at[place, me],
                send_sem=send_sem.at[slot],
                recv_sem=recv_sem.at[slot],
                device_id={"freq": peer},
                device_id_type=pl.DeviceIdType.MESH,
            ).start()
            return carry

        lax.fori_loop(1, devices, send, 0)
        targets[place, me] = sources[place, me]

    def await_all(phase, c, refs, sems):
        whole = refs.at[(phase // 2) * chunks + c, pl.ds(0, devices - 1)]
        pltpu.make_async_copy(whole, whole, sems.at[phase * chunks + c]).wait()

    def rim(place, side):
        return pltpu.make_async_remote_copy(
            src_ref=rim_out.at[place, side],
            dst_ref=rim_in.at[place, side],
            send_sem=rim_send.at[place, side],
            recv_sem=rim_recv.at[place, side],
            device_id={"freq": lax.rem(me + (1 if side == 0 else devices - 1), devices)},
            device_id_type=pl.DeviceIdType.MESH,
        )

    sends = (me < devices - 1, me > 0)
    gets = (me > 0, me < devices - 1)

    def analyse(s, samples):
        both = nt_dot(analysis_ref[...], samples)
        wide[pl.ds(s, rows, stride=local_src), :] = both[:rows] + both[rows:]

    def ship(sweep, c):
        slabs = wide[...].reshape(devices, local_freq * 2 * local_src, width)
        out_slabs[sweep * chunks + c] = slabs.astype(BF16)
        if sweep == 0 and c == 0:
            pl.semaphore_wait(barrier, devices - 1)
        exchange(2 * sweep, c, out_slabs, in_slabs)

    def own(sweep, c):
        await_all(2 * sweep, c, in_slabs, recv_sem)
        arrived = in_slabs[sweep * chunks + c].astype(F32)
        backs = []
        for f in range(local_freq):
            part = arrived[:, f * 2 * local_src : (f + 1) * 2 * local_src]
            owned = part.reshape(devices * 2 * local_src, width).T.astype(BF16)
            predicted = jnp.dot(owned, inner[f], preferred_element_type=F32)
            given[...] = recorded_ref[f, pl.ds(c * width * NB, width * NB), :].astype(F32)
            narrow = []
            for j in range(NB):
                left = given[pl.ds(j, width, stride=NB), :] - predicted[:, j * block_cols : (j + 1) * block_cols]
                if sweep == 1:
                    residual_ref[f, pl.ds(c * width * NB + j, width, stride=NB), :] = left
                narrow.append(left.astype(BF16))
            back = nt_dot(inner[f], jnp.concatenate(narrow, axis=1))
            backs.append(back.reshape(devices, 2 * local_src, width))
        back = backs[0] if local_freq == 1 else jnp.concatenate(backs, axis=1)
        back_slabs[sweep * chunks + c] = back.astype(BF16)
        exchange(2 * sweep + 1, c, back_slabs, edge_slabs)

    def trace_side(sweep, c):
        place = sweep * chunks + c
        await_all(2 * sweep + 1, c, edge_slabs, recv_sem)
        flat[...] = edge_slabs[place].astype(F32).reshape(rows * local_src, width)
        for s in range(local_src):
            near[RADIUS + s] = flat[pl.ds(s, rows, stride=local_src), :]
        rim_out[place, 0] = near[local_src : local_src + RADIUS].astype(BF16)
        rim_out[place, 1] = near[RADIUS : 2 * RADIUS].astype(BF16)
        for side in range(2):

            @pl.when(sends[side])
            def _():
                rim(place, side).start()

        span_lanes = pl.ds(c * width, width)

        def source(s, carry):
            span = spans[s, :, span_lanes]
            box = near[s + RADIUS]
            smoothed = box
            for offset in range(1, RADIUS + 1):
                box = box + (near[s + RADIUS + offset] + near[s + RADIUS - offset])
                smoothed = jnp.where(span >= offset, box, smoothed)
            smoothed = smoothed * (1.0 / (2.0 * span.astype(F32) + 1.0))
            high = smoothed.astype(BF16)
            low = (smoothed - high.astype(F32)).astype(BF16)
            stack = jnp.concatenate([high, low, high], axis=0)
            if sweep == 0:
                update = soft(field[c, s].astype(F32) + tn_dot(stack, synthesis_ref[...]))
                field_ref[s, span_lanes, :] = update
                analyse(s, update.astype(BF16))
            elif c < chunks - 1:
                field_ref[s, span_lanes, :] = soft(field_ref[s, span_lanes, :] + tn_dot(stack, synthesis_ref[...]))
            else:
                last_ref[s] = stack
            return carry

        low_end = min(RADIUS, local_src)
        high_end = max(local_src - RADIUS, low_end)
        lax.fori_loop(low_end, high_end, source, 0, unroll=2)
        for side in range(2):

            @pl.when(gets[side])
            def _():
                rim(place, side).wait_recv()
                at = 0 if side == 0 else RADIUS + local_src
                near[at : at + RADIUS] = rim_in[place, side].astype(F32)

        lax.fori_loop(0, low_end, source, 0, unroll=2)
        lax.fori_loop(high_end, local_src, source, 0, unroll=2)
        if sweep == 0:
            ship(1, c)

    for c in range(chunks):
        load(c).wait()

        def source(s, carry):
            analyse(s, field[c, s])
            return carry

        lax.fori_loop(0, local_src, source, 0, unroll=4)
        ship(0, c)
    build_operator(block_ref, multiples_ref, inner, local_src)
    near[...] = jnp.zeros_like(near)
    for s in range(local_src):
        spans[s] = radius_ref[s : s + 1, :]
    for c in range(chunks):
        own(0, c)
    for c in range(chunks):
        trace_side(0, c)
    for c in range(chunks):
        own(1, c)
    for c in range(chunks):
        trace_side(1, c)
    for phase in range(4):
        for c in range(chunks):
            await_all(phase, c, back_slabs if phase % 2 else out_slabs, send_sem)
    for place in range(2 * chunks):
        for side in range(2):

            @pl.when(sends[side])
            def _():
                rim(place, side).wait_send()


def finish_kernel(
    once_ref, last_ref, residual_ref, synthesis_ref, field_hbm, residual_hbm, done, ready_sem, done_sem, residual_sem
):
    local_src, receivers, _ = once_ref.shape
    width = last_ref.shape[2]
    start = receivers - width
    ready = pltpu.make_async_copy(once_ref.at[:, pl.ds(0, start), :], field_hbm.at[:, pl.ds(0, start), :], ready_sem)
    residual = pltpu.make_async_copy(residual_ref, residual_hbm, residual_sem)
    if start:
        ready.start()
    residual.start()

    def source(s, carry):
        done[s] = soft(once_ref[s, pl.ds(start, width), :] + tn_dot(last_ref[s], synthesis_ref[...]))
        pltpu.make_async_copy(done.at[s], field_hbm.at[s, pl.ds(start, width), :], done_sem).start()
        return carry

    lax.fori_loop(0, local_src, source, 0, unroll=2)
    pltpu.make_async_copy(done, field_hbm.at[:, pl.ds(start, width), :], done_sem).wait()
    residual.wait()
    if start:
        ready.wait()


def on_device(devices, start_field, recorded, multiples, block_index, radius):
    local_src, receivers, samples = start_field.shape
    local_freq = recorded.shape[0]
    rows = 2 * local_freq * devices
    width = 128
    chunks = receivers // width
    table = dft_table(local_freq * devices, samples)
    analysis = jnp.concatenate(halves(table.T), axis=0)
    high, low = halves(step_size * table.T)
    synthesis = jnp.concatenate([high, high, low], axis=0)
    vmem = pl.BlockSpec(memory_space=pltpu.VMEM)
    hbm = pl.BlockSpec(memory_space=pltpu.HBM)
    slab = pltpu.VMEM((2 * chunks, devices, local_freq * 2 * local_src, width), BF16)
    rim = pltpu.VMEM((2 * chunks, 2, RADIUS, rows, width), BF16)
    flat = pltpu.VMEM((rows * local_src, width), F32)
    field_shape = jax.ShapeDtypeStruct(start_field.shape, F32)
    residual_shape = jax.ShapeDtypeStruct((local_freq, receivers * NB, 2 * BS), F32)
    once, last, residual = pl.pallas_call(
        functools.partial(sweeps_kernel, devices, chunks, width),
        out_shape=(field_shape, jax.ShapeDtypeStruct((local_src, 3 * rows, width), BF16), residual_shape),
        in_specs=[pl.BlockSpec(memory_space=pltpu.SMEM), hbm] + [vmem] * 5,
        out_specs=(vmem, vmem, vmem),
        scratch_shapes=[
            pltpu.VMEM((chunks, local_src, width, samples), BF16),
            flat,
            flat,
            pltpu.VMEM((local_src + 2 * RADIUS, rows, width), F32),
            pltpu.VMEM((local_src, 1, receivers), jnp.int32),
            pltpu.VMEM((width * NB, 2 * BS), F32),
            pltpu.VMEM((local_freq, devices * 2 * local_src, NB * 2 * BS), BF16),
            slab,
            slab,
            slab,
            slab,
            rim,
            rim,
            pltpu.SemaphoreType.DMA((chunks,)),
            pltpu.SemaphoreType.DMA((4 * chunks,)),
            pltpu.SemaphoreType.DMA((4 * chunks,)),
            pltpu.SemaphoreType.DMA((2 * chunks, 2)),
            pltpu.SemaphoreType.DMA((2 * chunks, 2)),
        ],
        compiler_params=pltpu.CompilerParams(
            collective_id=0, has_side_effects=True, vmem_limit_bytes=28 << 20
        ),
    )(
        block_index, start_field, recorded.reshape(local_freq, receivers * NB, 2 * BS), multiples, radius,
        analysis, synthesis,
    )
    field, residual = pl.pallas_call(
        finish_kernel,
        out_shape=(field_shape, residual_shape),
        in_specs=[vmem] * 4,
        out_specs=(hbm, hbm),
        scratch_shapes=[
            pltpu.VMEM((local_src, width, samples), F32),
            pltpu.SemaphoreType.DMA,
            pltpu.SemaphoreType.DMA,
            pltpu.SemaphoreType.DMA,
        ],
        compiler_params=pltpu.CompilerParams(vmem_limit_bytes=24 << 20),
    )(once, last, residual, synthesis)
    return field, residual.reshape(recorded.shape)


def solution(mesh):
    placed = (
        P(("grp", "freq"), None, None),
        P(("grp", "freq"), None, None, None),
        P(("grp", "freq"), None, None, None, None),
        P(),
        P(("grp", "freq"), None),
    )
    return jax.shard_map(
        functools.partial(on_device, mesh.shape["freq"]),
        mesh=mesh,
        in_specs=placed,
        out_specs=(P(("grp", "freq"), None, None), P(("grp", "freq"), None, None, None)),
        check_vma=False,
    )
```

time: 82.2 us -> 73.6 us (0.90)
  the two profiles are of different devices: /device:TPU:25 before, /device:TPU:18 now
where the time goes in v2:
time: 73.6 us; the launch traced here: 73.2 us
  Pallas kernels  64.7 us (88%)
  local copies, waits for them, and re-layouts  7.85 us (11%)
    pallas_call x1, Pallas kernels, on_device(): pl.pallas_call(functools.partial(sweeps_kernel, devices, chunks, width),...  59.8 us
    unnamed x14, local copies, waits for them, and re-layouts  7.85 us
    pallas_call x1, Pallas kernels, on_device(): pl.pallas_call(finish_kernel, out_shape=(field_shape, residual_shape), in...  4.91 us

profile of v2, /device:TPU:18, one launch (start us, length us, event | category | flops | bytes accessed | tf_op | source)
XLA Modules:
  0.0 73.2 jit_solution(17834186825100915835)
XLA Ops:
  0.6 0.0 copy-start
  0.6 2.8 %copy-done = bf16[16,384,512]{2,1,0:T(8,128)(2,1)S(1)} copy-done((bf16[16,384,512]{2,1,0:T(8,128)(2,1)S(1)}, bf16[16,384,512]{2,1,0:T(8,128)(2,1)}, u32[]{:S(2)}) %copy-start) | copy-done | bytes 6291480
  3.4 0.0 copy-start.1
  3.4 0.9 %copy-done.1 = bf16[96,512]{1,0:T(8,128)(2,1)S(1)} copy-done((bf16[96,512]{1,0:T(8,128)(2,1)S(1)}, bf16[96,512]{1,0:T(8,128)(2,1)}, u32[]{:S(2)}) %copy-start.1) | copy-done | bytes 98328
  4.3 0.0 copy-start.2
  4.3 1.0 %copy-done.2 = bf16[1,384,4,128]{3,2,1,0:T(4,128)(2,1)S(1)} copy-done((bf16[1,384,4,128]{3,2,1,0:T(4,128)(2,1)S(1)}, bf16[1,384,4,128]{3,2,1,0:T(4,128)(2,1)}, u32[]{:S(2)}) %copy-start.2) | copy-done | bytes 393240
  5.3 0.0 copy-start.3
  5.3 0.9 %copy-done.3 = bf16[1,4,3,64,128]{4,3,2,1,0:T(8,128)(2,1)S(1)} copy-done((bf16[1,4,3,64,128]{4,3,2,1,0:T(8,128)(2,1)S(1)}, bf16[1,4,3,64,128]{4,3,2,1,0:T(8,128)(2,1)}, u32[]{:S(2)}) %copy-start.3) | copy-done | bytes 196632
  6.2 0.0 copy-start.4
  6.2 0.8 %copy-done.4 = bf16[64,512]{1,0:T(8,128)(2,1)S(1)} copy-done((bf16[64,512]{1,0:T(8,128)(2,1)S(1)}, bf16[64,512]{1,0:T(8,128)(2,1)}, u32[]{:S(2)}) %copy-start.4) | copy-done | bytes 65560
  7.1 0.0 copy-start.5
  7.1 0.7 %copy-done.5 = s32[16,384]{1,0:T(8,128)S(1)} copy-done((s32[16,384]{1,0:T(8,128)S(1)}, s32[16,384]{1,0:T(8,128)}, u32[]{:S(2)}) %copy-start.5) | copy-done | bytes 24600
  7.8 0.0 copy-start.6
  7.8 0.7 copy-done.6
  8.5 59.8 %shard_map.86 = (f32[16,384,512]{2,1,0:T(8,128)S(1)}, bf16[16,96,128]{2,1,0:T(8,128)(2,1)S(1)}, f32[1,1536,128]{2,1,0:T(8,128)S(1)}) custom-call(s32[4,3]{1,0:T(4,128)S(1)} %copy-done.6, bf16[16,384,512]{2,1,0:T(8,128)(2,1)S(1)} %copy-done, bf16[1,1536,128]{2,1,0:T(8,128)(2,1)S(1)} %bitcast.2, bf16[1,4,3,64,128]{4,3,2,1,0:T(8,128)(2,1)S(1)} %copy-done.3, ...), custom_call_target="tpu_custom_call" | custom-call | tf_op jit(solution)/shard_map/pallas_call | solution.py:285
  68.3 4.9 %shard_map.87 = (f32[16,384,512]{2,1,0:T(8,128)}, f32[1,1536,128]{2,1,0:T(8,128)}) custom-call(f32[16,384,512]{2,1,0:T(8,128)S(1)} %get-tuple-element.7.once_ref, bf16[16,96,128]{2,1,0:T(8,128)(2,1)S(1)} %get-tuple-element.8.last_ref, f32[1,1536,128]{2,1,0:T(8,128)S(1)} %get-tuple-element.9.residual_ref, bf16[96,512]{1,0:T(8,128)(2,1)S(1)} %copy-done.1), custom_call_target="tpu_custom_call" | custom-call | tf_op jit(solution)/shard_map/pallas_call | solution.py:317
Async XLA Ops:
  0.6 2.8 %copy-start = (bf16[16,384,512]{2,1,0:T(8,128)(2,1)S(1)}, bf16[16,384,512]{2,1,0:T(8,128)(2,1)}, u32[]{:S(2)}) copy-start(bf16[16,384,512]{2,1,0:T(8,128)(2,1)} %start_hbm.1) | copy-start | bytes 18874372
  3.4 0.9 %copy-start.1 = (bf16[96,512]{1,0:T(8,128)(2,1)S(1)}, bf16[96,512]{1,0:T(8,128)(2,1)}, u32[]{:S(2)}) copy-start(bf16[96,512]{1,0:T(8,128)(2,1)} %constant.19.synthesis_ref) | copy-start | bytes 294916
  4.3 1.0 %copy-start.2 = (bf16[1,384,4,128]{3,2,1,0:T(4,128)(2,1)S(1)}, bf16[1,384,4,128]{3,2,1,0:T(4,128)(2,1)}, u32[]{:S(2)}) copy-start(bf16[1,384,4,128]{3,2,1,0:T(4,128)(2,1)} %param.8) | copy-start | bytes 1179652
  5.3 0.9 %copy-start.3 = (bf16[1,4,3,64,128]{4,3,2,1,0:T(8,128)(2,1)S(1)}, bf16[1,4,3,64,128]{4,3,2,1,0:T(8,128)(2,1)}, u32[]{:S(2)}) copy-start(bf16[1,4,3,64,128]{4,3,2,1,0:T(8,128)(2,1)} %multiples_ref.1) | copy-start | bytes 589828
  6.2 0.8 %copy-start.4 = (bf16[64,512]{1,0:T(8,128)(2,1)S(1)}, bf16[64,512]{1,0:T(8,128)(2,1)}, u32[]{:S(2)}) copy-start(bf16[64,512]{1,0:T(8,128)(2,1)} %constant.14.analysis_ref) | copy-start | bytes 196612
  7.1 0.7 %copy-start.5 = (s32[16,384]{1,0:T(8,128)S(1)}, s32[16,384]{1,0:T(8,128)}, u32[]{:S(2)}) copy-start(s32[16,384]{1,0:T(8,128)} %radius_ref.1) | copy-start | bytes 73732
  7.8 0.7 copy-start.6

commit v3 on v2

--- a/solution.py
+++ b/solution.py
@@ -66,22 +66,40 @@
 
 def sweeps_kernel(
     devices, chunks, width,
-    block_ref, start_hbm, recorded_ref, multiples_ref, radius_ref, analysis_ref, synthesis_ref,
+    block_hbm, start_hbm, recorded_hbm, multiples_hbm, radius_hbm, analysis_hbm, synthesis_hbm,
     field_ref, last_ref, residual_ref,
     field, wide, flat, near, spans, given, inner, out_slabs, in_slabs, back_slabs, edge_slabs, rim_out, rim_in,
-    load_sem, send_sem, recv_sem, rim_send, rim_recv,
+    block_ref, recorded_ref, multiples_ref, radius_ref, analysis_ref, synthesis_ref,
+    load_sem, send_sem, recv_sem, rim_send, rim_recv, table_sem,
 ):
     me = lax.axis_index("freq")
     local_src = start_hbm.shape[0]
-    local_freq = multiples_ref.shape[0]
+    local_freq = multiples_hbm.shape[0]
     rows = analysis_ref.shape[0] // 2
     block_cols = 2 * BS
 
     def load(c):
         return pltpu.make_async_copy(start_hbm.at[:, pl.ds(c * width, width), :], field.at[c], load_sem.at[c])
 
-    for c in range(chunks):
+    load(0).start()
+    tables = [
+        pltpu.make_async_copy(source, target, table_sem.at[n])
+        for n, (source, target) in enumerate(
+            (
+                (analysis_hbm, analysis_ref),
+                (block_hbm, block_ref),
+                (multiples_hbm, multiples_ref),
+                (radius_hbm, radius_ref),
+                (recorded_hbm, recorded_ref),
+                (synthesis_hbm, synthesis_ref),
+            )
+        )
+    ]
+    tables[0].start()
+    for c in range(1, chunks):
         load(c).start()
+    for table in tables[1:]:
+        table.start()
     barrier = pltpu.get_barrier_semaphore()
     for shift in range(1, devices):
         pl.semaphore_signal(
@@ -195,7 +213,7 @@
 
         low_end = min(RADIUS, local_src)
         high_end = max(local_src - RADIUS, low_end)
-        lax.fori_loop(low_end, high_end, source, 0, unroll=2)
+        lax.fori_loop(low_end, high_end, source, 0, unroll=4)
         for side in range(2):
 
             @pl.when(gets[side])
@@ -204,11 +222,12 @@
                 at = 0 if side == 0 else RADIUS + local_src
                 near[at : at + RADIUS] = rim_in[place, side].astype(F32)
 
-        lax.fori_loop(0, low_end, source, 0, unroll=2)
-        lax.fori_loop(high_end, local_src, source, 0, unroll=2)
+        lax.fori_loop(0, low_end, source, 0, unroll=4)
+        lax.fori_loop(high_end, local_src, source, 0, unroll=4)
         if sweep == 0:
             ship(1, c)
 
+    tables[0].wait()
     for c in range(chunks):
         load(c).wait()
 
@@ -218,6 +237,8 @@
 
         lax.fori_loop(0, local_src, source, 0, unroll=4)
         ship(0, c)
+    for table in tables[1:]:
+        table.wait()
     build_operator(block_ref, multiples_ref, inner, local_src)
     near[...] = jnp.zeros_like(near)
     for s in range(local_src):
@@ -226,8 +247,9 @@
         own(0, c)
     for c in range(chunks):
         trace_side(0, c)
-    for c in range(chunks):
-        own(1, c)
+        if c:
+            own(1, c - 1)
+    own(1, chunks - 1)
     for c in range(chunks):
         trace_side(1, c)
     for phase in range(4):
@@ -242,23 +264,27 @@
 
 
 def finish_kernel(
-    once_ref, last_ref, residual_ref, synthesis_ref, field_hbm, residual_hbm, done, ready_sem, done_sem, residual_sem
+    once_ref, last_ref, residual_ref, synthesis_hbm, field_hbm, residual_hbm,
+    done, synthesis_ref, ready_sem, done_sem, residual_sem, table_sem,
 ):
     local_src, receivers, _ = once_ref.shape
     width = last_ref.shape[2]
     start = receivers - width
     ready = pltpu.make_async_copy(once_ref.at[:, pl.ds(0, start), :], field_hbm.at[:, pl.ds(0, start), :], ready_sem)
     residual = pltpu.make_async_copy(residual_ref, residual_hbm, residual_sem)
+    table = pltpu.make_async_copy(synthesis_hbm, synthesis_ref, table_sem)
+    table.start()
     if start:
         ready.start()
     residual.start()
+    table.wait()
 
     def source(s, carry):
         done[s] = soft(once_ref[s, pl.ds(start, width), :] + tn_dot(last_ref[s], synthesis_ref[...]))
         pltpu.make_async_copy(done.at[s], field_hbm.at[s, pl.ds(start, width), :], done_sem).start()
         return carry
 
-    lax.fori_loop(0, local_src, source, 0, unroll=2)
+    lax.fori_loop(0, local_src, source, 0, unroll=4)
     pltpu.make_async_copy(done, field_hbm.at[:, pl.ds(start, width), :], done_sem).wait()
     residual.wait()
     if start:
@@ -285,7 +311,7 @@
     once, last, residual = pl.pallas_call(
         functools.partial(sweeps_kernel, devices, chunks, width),
         out_shape=(field_shape, jax.ShapeDtypeStruct((local_src, 3 * rows, width), BF16), residual_shape),
-        in_specs=[pl.BlockSpec(memory_space=pltpu.SMEM), hbm] + [vmem] * 5,
+        in_specs=[hbm] * 7,
         out_specs=(vmem, vmem, vmem),
         scratch_shapes=[
             pltpu.VMEM((chunks, local_src, width, samples), BF16),
@@ -301,32 +327,46 @@
             slab,
             rim,
             rim,
+            pltpu.SMEM(block_index.shape, block_index.dtype),
+            pltpu.VMEM((local_freq, receivers * NB, 2 * BS), BF16),
+            pltpu.VMEM(multiples.shape, BF16),
+            pltpu.VMEM(radius.shape, radius.dtype),
+            pltpu.VMEM(analysis.shape, BF16),
+            pltpu.VMEM(synthesis.shape, BF16),
             pltpu.SemaphoreType.DMA((chunks,)),
             pltpu.SemaphoreType.DMA((4 * chunks,)),
             pltpu.SemaphoreType.DMA((4 * chunks,)),
             pltpu.SemaphoreType.DMA((2 * chunks, 2)),
             pltpu.SemaphoreType.DMA((2 * chunks, 2)),
+            pltpu.SemaphoreType.DMA((6,)),
         ],
         compiler_params=pltpu.CompilerParams(
             collective_id=0, has_side_effects=True, vmem_limit_bytes=28 << 20
         ),
     )(
-        block_index, start_field, recorded.reshape(local_freq, receivers * NB, 2 * BS), multiples, radius,
-        analysis, synthesis,
+        *(
+            pltpu.with_memory_space_constraint(value, pltpu.HBM)
+            for value in (
+                block_index, start_field, recorded.reshape(local_freq, receivers * NB, 2 * BS), multiples, radius,
+                analysis, synthesis,
+            )
+        )
     )
     field, residual = pl.pallas_call(
         finish_kernel,
         out_shape=(field_shape, residual_shape),
-        in_specs=[vmem] * 4,
+        in_specs=[vmem] * 3 + [hbm],
         out_specs=(hbm, hbm),
         scratch_shapes=[
             pltpu.VMEM((local_src, width, samples), F32),
+            pltpu.VMEM(synthesis.shape, BF16),
+            pltpu.SemaphoreType.DMA,
             pltpu.SemaphoreType.DMA,
             pltpu.SemaphoreType.DMA,
             pltpu.SemaphoreType.DMA,
         ],
-        compiler_params=pltpu.CompilerParams(vmem_limit_bytes=24 << 20),
-    )(once, last, residual, synthesis)
+        compiler_params=pltpu.CompilerParams(vmem_limit_bytes=12 << 20),
+    )(once, last, residual, pltpu.with_memory_space_constraint(synthesis, pltpu.HBM))
     return field, residual.reshape(recorded.shape)
 
 

time: 73.6 us -> 60.3 us (0.82)
  local copies, waits for them, and re-layouts: 7.85 us -> 0 us
  Pallas kernels: 64.7 us -> 59.1 us
    unnamed x14 -> x0, local copies, waits for them, and re-layouts: 7.85 us -> none
    pallas_call x1, Pallas kernels: 59.8 us -> 54.2 us  [on_device(): pl.pallas_call(functools.partial(sweeps_kernel, devices, chunks, width),...]
where the time goes in v3:
time: 60.3 us; the launch traced here: 59.8 us
  Pallas kernels  59.1 us (98%)
  between operations  0.64 us (1%)
    pallas_call x1, Pallas kernels, on_device(): pl.pallas_call(functools.partial(sweeps_kernel, devices, chunks, width),...  54.2 us
    pallas_call x1, Pallas kernels, on_device(): pl.pallas_call(finish_kernel, out_shape=(field_shape, residual_shape), in...  4.92 us

profile of v3, /device:TPU:18, one launch (start us, length us, event | category | flops | bytes accessed | tf_op | source)
XLA Modules:
  0.0 59.8 jit_solution(15470580130187266805)
XLA Ops:
  0.6 54.2 %shard_map.86 = (f32[16,384,512]{2,1,0:T(8,128)S(1)}, bf16[16,96,128]{2,1,0:T(8,128)(2,1)S(1)}, f32[1,1536,128]{2,1,0:T(8,128)S(1)}) custom-call(s32[4,3]{1,0:T(4,128)} %block_hbm.1, bf16[16,384,512]{2,1,0:T(8,128)(2,1)} %start_hbm.1, bf16[1,1536,128]{2,1,0:T(8,128)(2,1)} %bitcast.2, bf16[1,4,3,64,128]{4,3,2,1,0:T(8,128)(2,1)} %multiples_hbm.1, ...), custom_call_target="tpu_custom_call" | custom-call | tf_op jit(solution)/shard_map/pallas_call | solution.py:311
  54.9 4.9 %shard_map.87 = (f32[16,384,512]{2,1,0:T(8,128)}, f32[1,1536,128]{2,1,0:T(8,128)}) custom-call(f32[16,384,512]{2,1,0:T(8,128)S(1)} %get-tuple-element.7.once_ref, bf16[16,96,128]{2,1,0:T(8,128)(2,1)S(1)} %get-tuple-element.8.last_ref, f32[1,1536,128]{2,1,0:T(8,128)S(1)} %get-tuple-element.9.residual_ref, bf16[96,512]{1,0:T(8,128)(2,1)} %constant.19.synthesis_hbm), custom_call_target="tpu_custom_call" | custom-call | tf_op jit(solution)/shard_map/pallas_call | solution.py:355

commit v4 on v3

--- a/solution.py
+++ b/solution.py
@@ -213,7 +213,7 @@
 
         low_end = min(RADIUS, local_src)
         high_end = max(local_src - RADIUS, low_end)
-        lax.fori_loop(low_end, high_end, source, 0, unroll=4)
+        lax.fori_loop(low_end, high_end, source, 0, unroll=8)
         for side in range(2):
 
             @pl.when(gets[side])
@@ -235,7 +235,7 @@
             analyse(s, field[c, s])
             return carry
 
-        lax.fori_loop(0, local_src, source, 0, unroll=4)
+        lax.fori_loop(0, local_src, source, 0, unroll=8)
         ship(0, c)
     for table in tables[1:]:
         table.wait()
@@ -284,7 +284,7 @@
         pltpu.make_async_copy(done.at[s], field_hbm.at[s, pl.ds(start, width), :], done_sem).start()
         return carry
 
-    lax.fori_loop(0, local_src, source, 0, unroll=4)
+    lax.fori_loop(0, local_src, source, 0, unroll=8)
     pltpu.make_async_copy(done, field_hbm.at[:, pl.ds(start, width), :], done_sem).wait()
     residual.wait()
     if start:

time: 60.3 us -> 62.4 us (1.035)
  Pallas kernels: 59.1 us -> 61.2 us
    pallas_call x1, Pallas kernels: 54.2 us -> 56.3 us  [on_device(): pl.pallas_call(functools.partial(sweeps_kernel, devices, chunks, width),...]
where the time goes in v4:
time: 62.4 us; the launch traced here: 61.8 us
  Pallas kernels  61.2 us (98%)
  between operations  0.64 us (1%)
    pallas_call x1, Pallas kernels, on_device(): pl.pallas_call(functools.partial(sweeps_kernel, devices, chunks, width),...  56.3 us
    pallas_call x1, Pallas kernels, on_device(): pl.pallas_call(finish_kernel, out_shape=(field_shape, residual_shape), in...  4.92 us

profile of v4, /device:TPU:18, one launch (start us, length us, event | category | flops | bytes accessed | tf_op | source)
XLA Modules:
  0.0 61.8 jit_solution(16825530047978375966)
XLA Ops:
  0.6 56.3 %shard_map.86 = (f32[16,384,512]{2,1,0:T(8,128)S(1)}, bf16[16,96,128]{2,1,0:T(8,128)(2,1)S(1)}, f32[1,1536,128]{2,1,0:T(8,128)S(1)}) custom-call(s32[4,3]{1,0:T(4,128)} %block_hbm.1, bf16[16,384,512]{2,1,0:T(8,128)(2,1)} %start_hbm.1, bf16[1,1536,128]{2,1,0:T(8,128)(2,1)} %bitcast.2, bf16[1,4,3,64,128]{4,3,2,1,0:T(8,128)(2,1)} %multiples_hbm.1, ...), custom_call_target="tpu_custom_call" | custom-call | tf_op jit(solution)/shard_map/pallas_call | solution.py:311
  56.9 4.9 %shard_map.87 = (f32[16,384,512]{2,1,0:T(8,128)}, f32[1,1536,128]{2,1,0:T(8,128)}) custom-call(f32[16,384,512]{2,1,0:T(8,128)S(1)} %get-tuple-element.7.once_ref, bf16[16,96,128]{2,1,0:T(8,128)(2,1)S(1)} %get-tuple-element.8.last_ref, f32[1,1536,128]{2,1,0:T(8,128)S(1)} %get-tuple-element.9.residual_ref, bf16[96,512]{1,0:T(8,128)(2,1)} %constant.19.synthesis_hbm), custom_call_target="tpu_custom_call" | custom-call | tf_op jit(solution)/shard_map/pallas_call | solution.py:355
